TPU v7x, 32 devices: a whole 2x2x4 slice. The times are simulated.
32 devices in a mesh: dp: 8 (over z, y), group: 4 (over x, core).
Axes of the slice: x: 2, y: 2, z: 4, core: 2. Of those that a mesh axis runs over, the one named last changes fastest.
Arguments:
- waveform: bfloat16 [128, 2560], P(('dp', 'group')), may hold values from -6 to 6
- lengths: int32 [128], P(('dp', 'group')), may hold values from 1280 to 2560
- packing: int32 [128], P(('dp', 'group')), may hold values from 0 to 15, as said below
- first_weight: bfloat16 [512, 10], P('dp'), may hold values from -2 to 2
- norm_gain: float32 [512], replicated, may hold values from 0.25 to 1.75
- norm_bias: float32 [512], replicated, may hold values from -3 to 3
- conv_weight: bfloat16 [512, 1536], P('dp'), may hold values from -0.15625 to 0.15625
- grad_features: bfloat16 [128, 255, 512], P(('dp', 'group')), may hold values from -0.25 to 0.25
Outputs:
- features: bfloat16 [128, 255, 512], P(('dp', 'group'))
- grad_conv: float32 [512, 1536], P('dp')
- grad_first: float32 [512, 10], P('dp')
- grad_gain: float32 [512], replicated
- grad_bias: float32 [512], replicated
Inputs may be any that keep to these rules, and one draw needn't show every extreme that they name: `packing`: within each index of dp the 16 rows form a permutation of the positions of that index's block; position p lies on the device of group index p // 4 of the same dp index. Each device sends an even number of its rows to each device of its group, at most 2 to one device, and exactly 2 to some.
All inputs are finite; a program needn't handle non-finite values.
Results may differ from a plain program's by a relative error of at most 0.0057.
Values may be sent and summed in bfloat16 or wider, within the bound.
A program may use at most 64 MiB of HBM per device.

v0:
```python
import jax
import jax.numpy as jnp
from jax import lax
from jax.sharding import PartitionSpec as P


def gelu_slope(values):
    return (
        0.5 * (1.0 + lax.erf(values * 0.7071067811865476))
        + values * jnp.exp(-0.5 * values * values) * 0.3989422804014327
    )


def tap_matrix(hidden, frames_second):
    row_count, frames_first, channels = hidden.shape
    zero_frame = jnp.zeros((row_count, 1, channels), hidden.dtype)
    paired = jnp.concatenate([hidden, zero_frame], axis=1).reshape(
        row_count, frames_second + 1, 2, channels
    )
    even_half = paired[:, :, 0]
    odd_half = paired[:, :, 1]
    stacked = jnp.concatenate(
        [even_half[:, :frames_second], odd_half[:, :frames_second], even_half[:, 1:]], axis=2
    )
    return stacked.reshape(row_count * frames_second, 3 * channels)


def spread_back(back_taps, row_count, frames_second, frames_first):
    first_tap = back_taps[0].reshape(row_count, frames_second, -1)
    middle_tap = back_taps[1].reshape(row_count, frames_second, -1)
    last_tap = back_taps[2].reshape(row_count, frames_second, -1)
    channels = first_tap.shape[2]
    zero_frame = jnp.zeros((row_count, 1, channels), jnp.float32)
    even_half = jnp.concatenate([first_tap, zero_frame], axis=1) + jnp.concatenate(
        [zero_frame, last_tap], axis=1
    )
    odd_half = jnp.concatenate([middle_tap, zero_frame], axis=1)
    joined = jnp.stack([even_half, odd_half], axis=2).reshape(
        row_count, 2 * frames_second + 2, channels
    )
    return joined[:, :frames_first]


def local(
    waveform, lengths, packing, first_weight, norm_gain, norm_bias, conv_weight, grad_features
):
    row_count, capacity = waveform.shape
    channels = norm_gain.shape[0]
    frames_first = capacity // 5 - 1
    frames_second = (capacity // 5 - 2) // 2
    groups = lax.axis_size("group")
    own_group = lax.axis_index("group")
    group_rows = groups * row_count
    all_pack, all_lengths = (
        lax.all_gather(packing, "group", axis=0, tiled=True),
        lax.all_gather(lengths, "group", axis=0, tiled=True),
    )
    target = all_pack // row_count
    slot_index = all_pack % row_count
    positions = jnp.arange(group_rows)
    source = positions // row_count
    same_source = source[:, None] == source[None, :]
    same_target = target[:, None] == target[None, :]
    before = positions[:, None] > positions[None, :]
    rank_among = jnp.sum((same_source & same_target & before).astype(jnp.int32), axis=1)
    arriving = target == own_group
    slot_ids = jnp.arange(row_count)
    choose_slot = (slot_index[None, :] == slot_ids[:, None]) & arriving[None, :]
    local_lengths = jnp.sum(jnp.where(choose_slot, all_lengths[None, :], 0), axis=1)
    per_peer = 2 * ((row_count + 2 * groups - 1) // (2 * groups))
    lane_ids = jnp.arange(per_peer)
    own_target = lax.dynamic_slice_in_dim(target, own_group * row_count, row_count)
    own_rank = lax.dynamic_slice_in_dim(rank_among, own_group * row_count, row_count)
    outgoing = (
        (own_target[None, None, :] == jnp.arange(groups)[:, None, None])
        & (own_rank[None, None, :] == lane_ids[None, :, None])
    ).astype(jnp.bfloat16)
    send_rows = jnp.einsum(
        "gkr,rs->gks", outgoing, waveform, preferred_element_type=jnp.float32
    ).astype(jnp.bfloat16)
    received = lax.all_to_all(send_rows, "group", split_axis=0, concat_axis=0, tiled=True)
    pick_slots = (
        choose_slot[:, :, None] & (rank_among[None, :, None] == lane_ids[None, None, :])
    ).astype(jnp.float32)
    pick_slots = jnp.sum(pick_slots.reshape(row_count, groups, row_count, per_peer), axis=2).astype(
        jnp.bfloat16
    )
    wave_rows = jnp.einsum(
        "lsk,skn->ln", pick_slots, received, preferred_element_type=jnp.float32
    ).astype(jnp.bfloat16)
    first_whole = lax.all_gather(first_weight, "dp", axis=0, tiled=True)
    in_length = jnp.arange(capacity)[None, :] < local_lengths[:, None]
    masked = jnp.where(in_length, wave_rows, jnp.zeros_like(wave_rows))
    blocks = masked.reshape(row_count, capacity // 5, 5)
    taps_first = jnp.concatenate([blocks[:, :-1], blocks[:, 1:]], axis=2).reshape(
        row_count * frames_first, 10
    )
    conv_first = lax.dot_general(
        taps_first, first_whole, (((1,), (1,)), ((), ())), preferred_element_type=jnp.float32
    )
    conv_first = conv_first.reshape(row_count, frames_first, channels)
    count_first = (local_lengths - 10) // 5 + 1
    count_second = (count_first - 3) // 2 + 1
    valid_first = (jnp.arange(frames_first)[None, :] < count_first[:, None]).astype(jnp.float32)[
        :, :, None
    ]
    valid_second = (jnp.arange(frames_second)[None, :] < count_second[:, None]).astype(jnp.float32)[
        :, :, None
    ]
    count_float = count_first.astype(jnp.float32)[:, None, None]
    row_mean = jnp.sum(conv_first * valid_first, axis=1, keepdims=True) / count_float
    centred = (conv_first - row_mean) * valid_first
    row_var = jnp.sum(centred * centred, axis=1, keepdims=True) / count_float
    inv_scale = lax.rsqrt(row_var + 1e-05)
    normed = (conv_first - row_mean) * inv_scale
    shifted = normed * norm_gain + norm_bias
    hidden = (jax.nn.gelu(shifted, approximate=False) * valid_first).astype(jnp.bfloat16)
    taps_second = tap_matrix(hidden, frames_second)
    conv_whole = lax.all_gather(conv_weight, "dp", axis=0, tiled=True)
    conv_second = lax.dot_general(
        taps_second, conv_whole, (((1,), (1,)), ((), ())), preferred_element_type=jnp.float32
    )
    conv_second = conv_second.reshape(row_count, frames_second, channels)
    features = (jax.nn.gelu(conv_second, approximate=False) * valid_second).astype(jnp.bfloat16)
    delta_second = (
        grad_features.astype(jnp.float32) * valid_second * gelu_slope(conv_second)
    ).astype(jnp.bfloat16)
    delta_flat = delta_second.reshape(row_count * frames_second, channels)
    back_taps = tuple(
        (
            jnp.dot(
                delta_flat,
                conv_whole[:, tap_index * channels : (tap_index + 1) * channels],
                preferred_element_type=jnp.float32,
            )
            for tap_index in range(3)
        )
    )
    share = lax.psum_scatter(
        lax.dot_general(
            delta_flat, taps_second, (((0,), (0,)), ((), ())), preferred_element_type=jnp.float32
        ),
        "dp",
        scatter_dimension=0,
        tiled=True,
    )
    grad_conv = lax.psum(share, "group")
    delta_hidden = spread_back(back_taps, row_count, frames_second, frames_first)
    delta_norm = delta_hidden * valid_first * gelu_slope(shifted)
    gain_term = jnp.sum(delta_norm * normed, axis=(0, 1))
    bias_term = jnp.sum(delta_norm, axis=(0, 1))
    scaled = delta_norm * norm_gain
    mean_grad = jnp.sum(scaled, axis=1, keepdims=True) / count_float
    mean_cross = jnp.sum(scaled * normed, axis=1, keepdims=True) / count_float
    delta_first = ((scaled - mean_grad - normed * mean_cross) * inv_scale * valid_first).astype(
        jnp.bfloat16
    )
    first_term = lax.dot_general(
        delta_first.reshape(row_count * frames_first, channels),
        taps_first,
        (((0,), (0,)), ((), ())),
        preferred_element_type=jnp.float32,
    )
    stacked = jnp.concatenate([first_term, gain_term[:, None], bias_term[:, None]], axis=1)
    summed = lax.psum(stacked, ("dp", "group"))
    shard_rows = channels // lax.axis_size("dp")
    grad_first = lax.dynamic_slice_in_dim(
        summed[:, :10], lax.axis_index("dp") * shard_rows, shard_rows, 0
    )
    return (features, grad_conv, grad_first, summed[:, 10], summed[:, 11])


def solution(mesh):
    return jax.shard_map(
        local,
        mesh=mesh,
        in_specs=(
            P(("dp", "group"), None),
            P(("dp", "group")),
            P(("dp", "group")),
            P("dp", None),
            P(),
            P(),
            P("dp", None),
            P(("dp", "group"), None, None),
        ),
        out_specs=(P(("dp", "group"), None, None), P("dp", None), P("dp", None), P(), P()),
        check_vma=False,
    )
```

profile of v0, /device:TPU:0, one launch (start us, length us, event | category | flops | bytes accessed | tf_op | source)
XLA Modules:
  0.0 210.4 jit_solution(2185405149943320980)
XLA Ops:
  7.2 0.7 all-gather.3.cloned.1.call-update
  7.9 1.2 dynamic-slice
  9.8 0.9 dynamic-update-slice
  10.7 0.8 dynamic-update-slice.1
  11.5 6.4 %all-reduce.6 = (s32[16]{0:T(128)S(1)}, s32[16]{0:T(128)S(1)}) all-reduce(s32[16]{0:T(128)S(1)} %dynamic-update-slice, s32[16]{0:T(128)S(1)} %dynamic-update-slice.1), channel_id=1, replica_groups=mesh['dp'=8,'group'=4] {'group'}, use_global_device_ids=true, to_apply=%add.4 | all-reduce | flops 32 | bytes 256
  18.0 0.2 convert_reduce_fusion.1
  18.3 0.1 convolution_convert_fusion
  18.4 0.6 copy.42
  19.1 3.3 %all-to-all-start = ((bf16[4,2,2560]{2,1,0:T(2,128)(2,1)}), bf16[4,2,2560]{2,1,0:T(2,128)(2,1)S(1)}, u32[]{:S(2)}, u32[]{:S(2)}) async-start(bf16[4,2,2560]{2,1,0:T(2,128)(2,1)} %copy.42), calls=%async_computation | async-start | bytes 81920 | tf_op jit(solution)/shard_map/all_to_all | solution.py:81
  22.5 0.1 and.114
  22.7 0.1 select_reduce_fusion
  23.0 0.1 convert_reduce_fusion
  23.1 0.1 copy.54
  23.2 31.5 %all-gather = bf16[8,64,10]{1,2,0:T(8,128)(2,1)S(1)} all-gather(bf16[1,64,10]{1,2,0:T(8,128)(2,1)} %bitcast.60), channel_id=1, replica_groups=mesh['dp'=8,'group'=4] {'dp'}, dimensions={0}, use_global_device_ids=true | all-gather | bytes 11520 | tf_op jit(solution)/shard_map/all_gather | solution.py:91
  54.8 0.1 reshape.344
  54.8 0.2 fusion.17
  55.1 1.0 reshape.327
  56.1 0.2 fusion.61
  56.3 0.2 copy.58
  56.5 0.2 copy.59
  56.8 1.0 multiply_reduce_fusion.3
  57.9 0.7 multiply_reduce_fusion.2
  58.7 10.2 %fusion.3 = bf16[4,511,512]{2,1,0:T(8,128)(2,1)S(1)} fusion(f32[4,511,512]{2,1,0:T(8,128)S(1)} %get-tuple-element.51, f32[512]{0:T(512)S(1)} %copy-done.5, f32[512]{0:T(512)S(1)} %copy-done.6, f32[4,512]{1,0:T(4,128)S(1)} %add_rsqrt_fusion, f32[4,512]{1,0:T(4,128)S(1)} %broadcast_divide_fusion.2, f32[4,511]{1,0:T(4,128)S(1)} %fusion.46), kind=kLoop, calls=%fused_computation.5 | loop fusion | flops 73256960 | bytes 6307824 | tf_op jit(solution)/shard_map/convert_element_type | solution.py:117
  68.9 1.5 concatenate.22
  70.4 2.7 %reshape.328 = bf16[4,256,2,512]{3,2,1,0:T(2,128)(2,1)S(1)} reshape(bf16[4,512,512]{2,1,0:T(8,128)(2,1)} %concatenate.22) | data formatting | bytes 4194304 | tf_op jit(solution)/shard_map/reshape | solution.py:17
  73.2 3.0 %fusion.59 = (bf16[4,256,1,512]{3,2,1,0:T(2,128)(2,1)S(1)}, bf16[4,256,1,512]{3,2,1,0:T(2,128)(2,1)S(1)}) fusion(bf16[4,256,2,512]{3,2,1,0:T(2,128)(2,1)S(1)} %reshape.328), kind=kLoop, calls=%fused_computation.134 | loop fusion | bytes 4194304 | tf_op jit(solution)/shard_map/slice | solution.py:21
  76.2 0.3 copy.65
  76.4 0.3 copy.66
  76.7 1.3 fusion.60
  78.1 10.2 %fusion.27 = (bf16[4,255,512]{2,1,0:T(8,128)(2,1)S(1)}, bf16[4,255,512]{2,1,0:T(8,128)(2,1)}) fusion(bf16[4,255,512]{2,0,1:T(4,128)(2,1)} %param.15, f32[4,255]{1,0:T(4,128)S(1)} %fusion.47, bf16[512,1536]{1,0:T(8,128)(2,1)} %all-gather.3.cloned.1.call-done, bf16[4,255,512]{2,1,0:T(8,128)(2,1)} %get-tuple-element.41, bf16[4,255,512]{2,1,0:T(8,128)(2,1)S(1)} %bitcast.55, ...), kind=kOutput, calls=%fused_computation.53 | convolution fusion | flops 1654456320 | bytes 7843824 | tf_op jit(solution)/shard_map/dot_general | solution.py:120
  88.3 3.5 %convolution_bitcast_fusion.1 = f32[512,1536]{1,0:T(8,128)} fusion(bf16[4,255,512]{2,1,0:T(8,128)(2,1)S(1)} %get-tuple-element.36, bf16[4,255,512]{2,1,0:T(8,128)(2,1)S(1)} %copy-done.4, bf16[4,255,512]{2,1,0:T(8,128)(2,1)S(1)} %bitcast.56, bf16[4,255,512]{2,1,0:T(8,128)(2,1)S(1)} %get-tuple-element.40), kind=kOutput, calls=%fused_computation.40 | convolution fusion | flops 1613721600 | bytes 7323648 | tf_op jit(solution)/shard_map/dot_general | solution.py:140
  91.8 0.2 all-reduce.9.cloned.1.call-start
  92.0 3.1 %copy.53 = bf16[4,255,512]{2,0,1:T(4,128)(2,1)} copy(bf16[4,255,512]{2,1,0:T(8,128)(2,1)} %get-tuple-element.37) | data formatting | bytes 2088960
  95.2 0.7 fusion.39
  95.9 0.7 fusion.40
  96.6 0.7 fusion.41
  97.3 1.0 pad_bitcast_fusion
  98.3 0.7 pad_maximum_fusion
  99.0 5.2 %copy.52 = f32[4,256,2,512]{3,2,1,0:T(2,128)} copy(f32[4,256,2,512]{3,1,0,2:T(8,128)S(1)} %pad_maximum_fusion) | data formatting | bytes 8388608 | tf_op jit(solution)/shard_map/stack | solution.py:38
  104.2 6.1 %reshape.329 = f32[4,512,512]{2,1,0:T(8,128)} reshape(f32[4,256,2,512]{3,2,1,0:T(2,128)} %copy.52) | data formatting | bytes 8388608 | tf_op jit(solution)/shard_map/reshape | solution.py:38
  110.3 6.1 %multiply_reduce_fusion.1 = (f32[4,512]{1,0:T(4,128)S(1)}, f32[512]{0:T(512)S(1)}, f32[4,512]{1,0:T(4,128)S(1)}, f32[512]{0:T(512)S(1)}, f32[4,511,512]{2,1,0:T(8,128)S(1)}) fusion(f32[4,511,512]{2,1,0:T(8,128)} %copy-done.1, f32[512]{0:T(512)S(1)} %copy-done.6, f32[4,512]{1,0:T(4,128)S(1)} %add_rsqrt_fusion, f32[4,512]{1,0:T(4,128)S(1)} %broadcast_divide_fusion.2, ...), kind=kLoop, calls=%fused_computation.15 | loop fusion | flops 21971968 | bytes 12607472 | tf_op jit(solution)/shard_map/reduce_sum | solution.py:154
  116.4 1.3 fusion.38
  117.8 40.1 %psum.15 = f32[512,12]{0,1:T(8,128)S(1)} all-reduce(f32[512,12]{0,1:T(8,128)S(1)} %pad_maximum_fusion.7), channel_id=1, replica_groups=mesh['dp'=8,'group'=4] {'dp','group'}, use_global_device_ids=true, to_apply=%region_11.12 | all-reduce | flops 6144 | bytes 49152 | tf_op jit(solution)/shard_map/psum | solution.py:165
  157.9 0.7 constant_dynamic-slice_fusion
  158.6 9.3 %reduce-scatter.2.cloned.1.call-done = f32[64,1536]{1,0:T(8,128)} async-done(((f32[512,1536]{1,0:T(8,128)}), f32[64,1536]{1,0:T(8,128)}) %reduce-scatter.2.cloned.1.call-update) | async-done | bytes 393232 | tf_op jit(solution)/shard_map/reduce_scatter | solution.py:139
  168.0 0.6 fusion.62
  168.5 33.6 %all-reduce.9.cloned.1.call-done = f32[64,1536]{1,0:T(8,128)} async-done(((f32[64,1536]{1,0:T(8,128)}), f32[64,1536]{1,0:T(8,128)}) %all-reduce.9.cloned.1.call-update) | async-done | bytes 393232 | tf_op jit(solution)/shard_map/psum | solution.py:147
  202.1 1.8 copy.72
  (42 shorter events, 0.9 us)
Async XLA Ops:
  7.2 11.1 %copy-start = (bf16[4,2560]{1,0:T(4,128)(2,1)S(1)}, bf16[4,2560]{1,0:T(4,128)(2,1)}, u32[]{:S(2)}) copy-start(bf16[4,2560]{1,0:T(4,128)(2,1)} %param.8) | copy-start | bytes 61444
  7.2 70.9 %all-gather.3.cloned.1.call-start = ((), (), s32[]{:S(2)}) async-start(), calls=%async_computation.2 | async-start | bytes 1769472 | tf_op jit(solution)/shard_map/all_gather | solution.py:119
  19.1 35.8 %all-to-all-start = ((bf16[4,2,2560]{2,1,0:T(2,128)(2,1)}), bf16[4,2,2560]{2,1,0:T(2,128)(2,1)S(1)}, u32[]{:S(2)}, u32[]{:S(2)}) async-start(bf16[4,2,2560]{2,1,0:T(2,128)(2,1)} %copy.42), calls=%async_computation | async-start | bytes 81920 | tf_op jit(solution)/shard_map/all_to_all | solution.py:81
  22.4 145.6 %reduce-scatter.2.cloned.1.call-start = ((), (), s32[]{:S(2)}) async-start(), calls=%async_computation.3 | async-start | bytes 3538944 | tf_op jit(solution)/shard_map/reduce_scatter | solution.py:139
  56.7 1.9 copy-start.5
  56.8 1.9 copy-start.6
  57.8 11.1 %copy-start.1 = (f32[4,511,512]{2,1,0:T(8,128)}, f32[4,511,512]{2,1,0:T(8,128)S(1)}, u32[]{:S(2)}) copy-start(f32[4,511,512]{2,1,0:T(8,128)S(1)} %get-tuple-element.51) | copy-start | bytes 12558340
  78.1 10.2 %copy-start.4 = (bf16[4,255,512]{2,1,0:T(8,128)(2,1)S(1)}, bf16[4,255,512]{2,1,0:T(8,128)(2,1)}, u32[]{:S(2)}) copy-start(bf16[4,255,512]{2,1,0:T(8,128)(2,1)} %get-tuple-element.41) | copy-start | bytes 3133444
  91.8 3.4 %copy-start.3 = (bf16[512,1536]{1,0:T(8,128)(2,1)S(1)}, bf16[512,1536]{1,0:T(8,128)(2,1)}, u32[]{:S(2)}) copy-start(bf16[512,1536]{1,0:T(8,128)(2,1)} %all-gather.3.cloned.1.call-done) | copy-start | bytes 4718596
  91.8 110.3 %all-reduce.9.cloned.1.call-start = ((), (), s32[]{:S(2)}) async-start(), calls=%async_computation.4 | async-start | bytes 786432 | tf_op jit(solution)/shard_map/psum | solution.py:147
  110.3 6.1 %copy-start.2 = (f32[4,511,512]{2,1,0:T(8,128)S(1)}, f32[4,511,512]{2,1,0:T(8,128)}, u32[]{:S(2)}) copy-start(f32[4,511,512]{2,1,0:T(8,128)} %copy-done.1) | copy-start | bytes 12558340
Sparse Core Ops, SparseCore 0:
  10.2 47.2 all-gather.2
  91.9 75.9 reduce-scatter.1
  170.3 31.7 all-reduce.8
where the time goes:
time: 211 us; the launch traced here: 210 us
  blocking collectives  78 us (37%)
  waiting for transfers between devices  43.6 us (21%)
  local copies, waits for them, and re-layouts  32.4 us (15%)
  other arithmetic  19.6 us (9%)
  matrix products  18.5 us (9%)
  between operations  14.7 us (7%)
  starting transfers between devices  3.57 us (2%)
    psum x1, blocking collectives, local(): summed = lax.psum(stacked, ('dp', 'group'))  40.1 us
    psum x1, waiting for transfers between devices, local(): grad_conv = lax.psum(share, 'group')  33.6 us
    all_gather x1, blocking collectives, local(): first_whole = lax.all_gather(first_weight, 'dp', axis=0, tiled=True)  31.5 us
    convert_element_type x1, other arithmetic, local(): (jax.nn.gelu(shifted, approximate=False) * valid_first).astype(jnp.bfloat16)  10.2 us
    dot_general x1, matrix products, local(): lax.dot_general(taps_second, conv_whole, (((1,), (1,)), ((), ())), prefer...  10.2 us
    reduce_scatter x1, waiting for transfers between devices, local(): lax.psum_scatter(lax.dot_general(delta_flat, taps_second, (((0,), (0,)),...  9.35 us
    unnamed x26, local copies, waits for them, and re-layouts  9.01 us
    unnamed x1, blocking collectives  6.38 us
  transfers between devices with their start and end apart: 4, of which 2 were waited for; matrix products, arithmetic and copies ran while one was open for 26% of the time, Pallas kernels for 0%

commit v1 on v0

--- a/solution.py
+++ b/solution.py
@@ -1,7 +1,15 @@
+import functools
+
 import jax
 import jax.numpy as jnp
 from jax import lax
+from jax.experimental import pallas as pl
+from jax.experimental.pallas import tpu as pltpu
 from jax.sharding import PartitionSpec as P
+
+MESH = pl.DeviceIdType.MESH
+F32, BF16 = jnp.float32, jnp.bfloat16
+STEP = 32
 
 
 def gelu_slope(values):
@@ -170,9 +178,412 @@
     return (features, grad_conv, grad_first, summed[:, 10], summed[:, 11])
 
 
+def phi_and_slope(values):
+    phi = 0.5 * (1.0 + lax.erf(values * 0.7071067811865476))
+    return phi, phi + values * jnp.exp(-0.5 * values * values) * 0.3989422804014327
+
+
+def fold_rows(block):
+    return jnp.sum(block.reshape(block.shape[0] // 8, 8, block.shape[1]), axis=0)
+
+
+def fused_kernel(
+    wave_ref, first_ref, conv_ref, gain_ref, bias_ref, cot_ref,
+    feat_ref, gconv_ref, small_ref,
+    rows_all, first_all, first_both, conv_all, normed, slope, taps, even_rows, delta, second,
+    cot_rows, feat_rows, lhs_all, counts, inv_all, back, dfirst, first_acc, sums,
+    gc_full, gc_send, gc_r1, gc_k2, gc_s2, gc_r2, gc_k3, gc_s3, gc_r3, gc_k4, gc_s4, gc_r4, gc_out,
+    sm_grp, sm_y, sm_z,
+    row_ss, row_rs, first_ss, first_rs, conv_ss, conv_rs, fwd_ss, fwd_rs, own_sem,
+    st_ss, st_rs, z_ss, z_rs, out_ss, out_rs, sg_ss, sg_rs, sy_ss, sy_rs, sz_ss, sz_rs,
+):
+    dp, grp = lax.axis_index("dp"), lax.axis_index("group")
+    core, xpos = grp % 2, grp // 2
+    ypos, zpos = dp % 2, dp // 2
+    partner = (dp, xpos * 2 + (1 - core))
+    xpeer = (dp, (1 - xpos) * 2 + core)
+    ypeer = (zpos * 2 + (1 - ypos), grp)
+
+    def remote(src, dst, ss, rs, dev):
+        return pltpu.make_async_remote_copy(
+            src_ref=src, dst_ref=dst, send_sem=ss, recv_sem=rs, device_id=dev, device_id_type=MESH
+        )
+
+    barrier = pltpu.get_barrier_semaphore()
+    for j in range(1, 4):
+        pl.semaphore_signal(barrier, inc=1, device_id=(dp, (grp + j) % 4), device_id_type=MESH)
+    for j in range(1, 8):
+        pl.semaphore_signal(barrier, inc=1, device_id=((dp + j) % 8, grp), device_id_type=MESH)
+    pl.semaphore_wait(barrier, 10)
+
+    row_sends = []
+    for j in range(1, 4):
+        c = remote(wave_ref, rows_all.at[grp], row_ss.at[j], row_rs.at[grp], (dp, (grp + j) % 4))
+        c.start()
+        row_sends.append(c)
+    first_sends, conv_sends = [], []
+    for j in range(1, 8):
+        c = remote(first_ref, first_all.at[dp], first_ss.at[j], first_rs.at[dp], ((dp + j) % 8, grp))
+        c.start()
+        first_sends.append(c)
+    for j in range(1, 8):
+        c = remote(
+            conv_ref.at[core], conv_all.at[dp, core], conv_ss.at[j], conv_rs.at[dp], ((dp + j) % 8, grp)
+        )
+        c.start()
+        conv_sends.append(c)
+    own = pltpu.make_async_copy(conv_ref, conv_all.at[dp], own_sem)
+    own.start()
+    rows_all[grp] = wave_ref[...]
+    first_all[dp] = first_ref[...]
+    cot_rows[240:256] = jnp.zeros((16, 512), BF16)
+    even_rows[256:264] = jnp.zeros((8, 512), F32)
+    first_acc[...] = jnp.zeros_like(first_acc)
+    sums[...] = jnp.zeros_like(sums)
+
+    for j in range(1, 4):
+        p = (grp + j) % 4
+        remote(wave_ref, rows_all.at[p], row_ss.at[j], row_rs.at[p], (dp, p)).wait_recv()
+    for j in range(1, 8):
+        p = (dp + j) % 8
+        remote(first_ref, first_all.at[p], first_ss.at[j], first_rs.at[p], (p, grp)).wait_recv()
+
+    for b in range(4):
+        joined = first_all[2 * b] + first_all[2 * b + 1]
+        lanes = slice(b * 128, b * 128 + 128)
+        first_both[0:16, lanes] = joined[0:16]
+        first_both[16:32, lanes] = jnp.zeros((16, 128), BF16)
+        first_both[:, 512 + b * 128 : 640 + b * 128] = joined[16:48]
+
+    def chunk(i):
+        return pl.ds(pl.multiple_of(i * STEP, STEP), STEP)
+
+    def frame_ids(i):
+        ids = lax.broadcasted_iota(jnp.int32, (STEP, 512), 0) + i * STEP
+        return ids.astype(F32)
+
+    steps = 256 // STEP
+
+    def front(r, _):
+        place = (grp * 4 + r).astype(F32)
+        chosen = jnp.zeros((16, 256), F32)
+        for s in range(4):
+            for i in range(4):
+                row = rows_all[s, i].astype(F32)
+                chosen = chosen + row * (row[10:11] == place).astype(F32)
+        lhs_all[r, 0:16] = chosen.astype(BF16)
+        lhs_all[r, 16:32] = pltpu.roll(chosen, 255, 1).astype(BF16)
+        length = chosen[11:12] * 16.0 + chosen[12:13]
+        length = jnp.concatenate([length, length], axis=1)
+        count = jnp.floor((length - 9.5) * 0.2) + 1.0
+        counts[r] = count
+        normed[r] = lax.dot_general(
+            lhs_all[r], first_both[...], (((0,), (0,)), ((), ())), preferred_element_type=F32
+        )
+        inv_count = 1.0 / count
+
+        def add_up(i, acc):
+            ids = frame_ids(i) * 2.0
+            even = jnp.where(ids < count, normed[r, chunk(i), 0:512], 0.0)
+            odd = jnp.where(ids + 1.0 < count, normed[r, chunk(i), 512:1024], 0.0)
+            return acc + fold_rows(even + odd)
+
+        total = lax.fori_loop(0, steps, add_up, jnp.zeros((8, 512), F32))
+        mean = jnp.sum(total, axis=0, keepdims=True) * inv_count
+
+        def add_squares(i, acc):
+            ids = frame_ids(i) * 2.0
+            even = jnp.where(ids < count, normed[r, chunk(i), 0:512] - mean, 0.0)
+            odd = jnp.where(ids + 1.0 < count, normed[r, chunk(i), 512:1024] - mean, 0.0)
+            return acc + fold_rows(even * even + odd * odd)
+
+        total = lax.fori_loop(0, steps, add_squares, jnp.zeros((8, 512), F32))
+        inv = lax.rsqrt(jnp.sum(total, axis=0, keepdims=True) * inv_count + 1e-05)
+        inv_all[r] = inv
+        gain, bias = gain_ref[...], bias_ref[...]
+
+        def activate(i, _):
+            ids = frame_ids(i) * 2.0
+            rows = pl.ds(pl.multiple_of(r * 256 + i * STEP, STEP), STEP)
+            for half in range(2):
+                cols = slice(half * 512, half * 512 + 512)
+                valid = ids + float(half) < count
+                value = (normed[r, chunk(i), cols] - mean) * inv
+                normed[r, chunk(i), cols] = value
+                shifted = value * gain + bias
+                phi, grad = phi_and_slope(shifted)
+                hidden = jnp.where(valid, shifted * phi, 0.0)
+                slope[r, chunk(i), cols] = jnp.where(valid, grad, 0.0)
+                taps[rows, cols] = hidden.astype(BF16)
+                if half == 0:
+                    even_rows[chunk(i)] = hidden
+            return 0
+
+        lax.fori_loop(0, steps, activate, 0)
+        all_rows = pl.ds(pl.multiple_of(r * 256, 256), 256)
+        taps[all_rows, 1024:1536] = even_rows[1:257].astype(BF16)
+        return 0
+
+    lax.fori_loop(0, 4, front, 0)
+
+    forwards = []
+    for j in range(1, 8):
+        p = (dp + j) % 8
+        remote(conv_ref.at[core], conv_all.at[p, core], conv_ss.at[j], conv_rs.at[p], (p, grp)).wait_recv()
+        c = remote(conv_all.at[p, core], conv_all.at[p, core], fwd_ss.at[j], fwd_rs.at[p], partner)
+        c.start()
+        forwards.append(c)
+    own.wait()
+    for j in range(1, 8):
+        p = (dp + j) % 8
+        other = conv_all.at[p, 1 - core]
+        remote(other, other, fwd_ss.at[j], fwd_rs.at[p], partner).wait_recv()
+
+    def middle(r, _):
+        all_rows = pl.ds(pl.multiple_of(r * 256, 256), 256)
+        second[...] = lax.dot_general(
+            taps[all_rows, :],
+            conv_all[...].reshape(512, 1536),
+            (((1,), (1,)), ((), ())),
+            preferred_element_type=F32,
+        )
+        cot_rows[0:255] = cot_ref[r]
+        count2 = jnp.floor((counts[r] - 2.5) * 0.5) + 1.0
+
+        def activate(i, _):
+            valid = frame_ids(i) < count2
+            value = second[chunk(i)]
+            phi, grad = phi_and_slope(value)
+            feat_rows[chunk(i)] = jnp.where(valid, value * phi, 0.0).astype(BF16)
+            rows = pl.ds(pl.multiple_of(r * 256 + i * STEP, STEP), STEP)
+            delta[rows, :] = jnp.where(valid, cot_rows[chunk(i)].astype(F32) * grad, 0.0).astype(BF16)
+            return 0
+
+        lax.fori_loop(0, steps, activate, 0)
+        feat_ref[r] = feat_rows[0:255]
+        return 0
+
+    lax.fori_loop(0, 4, middle, 0)
+
+    def weight_grad(m, _):
+        cols = pl.ds(pl.multiple_of(m * 128, 128), 128)
+        part = lax.dot_general(
+            delta[:, cols], taps[...], (((0,), (0,)), ((), ())), preferred_element_type=F32
+        ).reshape(2, 2, 2, 16, 1536)
+        gc_full[pl.ds(m * 2, 2)] = part
+        gc_send[pl.ds(m * 2, 2)] = part.astype(BF16)
+        return 0
+
+    lax.fori_loop(0, 4, weight_grad, 0)
+    stage1 = remote(gc_send.at[:, :, 1 - core], gc_r1, st_ss.at[0], st_rs.at[0], partner)
+    stage1.start()
+
+    def backward(r):
+        rows = slice(r * 256, r * 256 + 256)
+        weights = conv_all[...].reshape(512, 1536)
+        part = lax.dot_general(
+            delta[rows, :], weights[:, 0:1024], (((1,), (0,)), ((), ())), preferred_element_type=F32
+        )
+        back[8:264, :] = part
+        even_rows[0:8] = jnp.zeros((8, 512), F32)
+        even_rows[8:264] = lax.dot_general(
+            delta[rows, :], weights[:, 1024:1536], (((1,), (0,)), ((), ())), preferred_element_type=F32
+        )
+        back[8:264, 0:512] = back[8:264, 0:512] + even_rows[7:263]
+        count, inv, gain = counts[r], inv_all[r], gain_ref[...]
+        inv_count = 1.0 / count
+
+        def shifted_chunk(i):
+            return pl.ds(pl.multiple_of(i * STEP + 8, 8), STEP)
+
+        def norm_sums(i, carry):
+            plain, cross = carry
+            even = back[shifted_chunk(i), 0:512] * slope[r, chunk(i), 0:512]
+            odd = back[shifted_chunk(i), 512:1024] * slope[r, chunk(i), 512:1024]
+            back[shifted_chunk(i), 0:512] = even
+            back[shifted_chunk(i), 512:1024] = odd
+            both = even * normed[r, chunk(i), 0:512] + odd * normed[r, chunk(i), 512:1024]
+            return plain + fold_rows(even + odd), cross + fold_rows(both)
+
+        zero = jnp.zeros((8, 512), F32)
+        plain, cross = lax.fori_loop(0, steps, norm_sums, (zero, zero))
+        plain = jnp.sum(plain, axis=0, keepdims=True)
+        cross = jnp.sum(cross, axis=0, keepdims=True)
+        sums[0:1] = sums[0:1] + cross
+        sums[1:2] = sums[1:2] + plain
+        mean_grad = plain * gain * inv_count
+        mean_cross = cross * gain * inv_count
+
+        def first_delta(i, _):
+            ids = frame_ids(i) * 2.0
+            for half in range(2):
+                cols = slice(half * 512, half * 512 + 512)
+                value = back[shifted_chunk(i), cols] * gain - mean_grad
+                value = (value - normed[r, chunk(i), cols] * mean_cross) * inv
+                dfirst[chunk(i), cols] = jnp.where(ids + float(half) < count, value, 0.0).astype(BF16)
+            return 0
+
+        lax.fori_loop(0, steps, first_delta, 0)
+        first_acc[...] += lax.dot_general(
+            lhs_all[r], dfirst[...], (((1,), (0,)), ((), ())), preferred_element_type=F32
+        )
+
+    backward(0)
+
+    stage1.wait()
+
+    def reduce_core(d, _):
+        gc_k2[d] = gc_full[d, xpos, core] + gc_r1[d, xpos].astype(F32)
+        gc_s2[d] = (gc_full[d, 1 - xpos, core] + gc_r1[d, 1 - xpos].astype(F32)).astype(BF16)
+        return 0
+
+    lax.fori_loop(0, 8, reduce_core, 0)
+    stage2 = remote(gc_s2, gc_r2, st_ss.at[1], st_rs.at[1], xpeer)
+    stage2.start()
+
+    backward(1)
+    backward(2)
+    stage2.wait()
+
+    def reduce_x(z, _):
+        keep, give = z * 2 + ypos, z * 2 + 1 - ypos
+        gc_k3[z] = gc_k2[keep] + gc_r2[keep].astype(F32)
+        gc_s3[z] = (gc_k2[give] + gc_r2[give].astype(F32)).astype(BF16)
+        return 0
+
+    lax.fori_loop(0, 4, reduce_x, 0)
+    stage3 = remote(gc_s3, gc_r3, st_ss.at[2], st_rs.at[2], ypeer)
+    stage3.start()
+
+    backward(3)
+
+    small = sm_grp.at[grp]
+    small[0:10] = first_acc[0:10, 0:512]
+    small[0:5] = small[0:5] + first_acc[5:10, 512:1024]
+    small[5:10] = small[5:10] + first_acc[16:21, 512:1024]
+    small[10:12] = sums[0:2]
+    small[12:16] = jnp.zeros((4, 512), F32)
+    sg = []
+    for j in range(1, 4):
+        c = remote(sm_grp.at[grp], sm_grp.at[grp], sg_ss.at[j], sg_rs.at[grp], (dp, (grp + j) % 4))
+        c.start()
+        sg.append(c)
+
+    stage3.wait()
+
+    def reduce_y(z, _):
+        total = gc_k3[z] + gc_r3[z].astype(F32)
+        gc_k4[z] = total
+        gc_s4[z] = total.astype(BF16)
+        return 0
+
+    lax.fori_loop(0, 4, reduce_y, 0)
+    zs = []
+    for j in range(1, 4):
+        zp = (zpos + j) % 4
+        c = remote(gc_s4.at[zp], gc_r4.at[zpos], z_ss.at[j], z_rs.at[zpos], (zp * 2 + ypos, grp))
+        c.start()
+        zs.append(c)
+
+    for j in range(1, 4):
+        p = (grp + j) % 4
+        remote(sm_grp.at[p], sm_grp.at[p], sg_ss.at[j], sg_rs.at[p], (dp, p)).wait_recv()
+    sm_y[0] = (sm_grp[0] + sm_grp[1]) + (sm_grp[2] + sm_grp[3])
+    sy = remote(sm_y.at[0], sm_y.at[1], sy_ss, sy_rs, ypeer)
+    sy.start()
+
+    total = gc_k4[zpos]
+    for j in range(1, 4):
+        zp = (zpos + j) % 4
+        remote(gc_s4.at[zp], gc_r4.at[zp], z_ss.at[j], z_rs.at[zp], (zp * 2 + ypos, grp)).wait_recv()
+    for j in range(1, 4):
+        total = total + gc_r4[(zpos + j) % 4].astype(F32)
+    gc_out[grp] = total
+    outs = []
+    for j in range(1, 4):
+        c = remote(gc_out.at[grp], gc_out.at[grp], out_ss.at[j], out_rs.at[grp], (dp, (grp + j) % 4))
+        c.start()
+        outs.append(c)
+
+    sy.wait()
+    sm_z[zpos] = sm_y[0] + sm_y[1]
+    sz = []
+    for j in range(1, 4):
+        zp = (zpos + j) % 4
+        c = remote(sm_z.at[zpos], sm_z.at[zpos], sz_ss.at[j], sz_rs.at[zpos], (zp * 2 + ypos, grp))
+        c.start()
+        sz.append(c)
+    for j in range(1, 4):
+        p = (grp + j) % 4
+        remote(gc_out.at[p], gc_out.at[p], out_ss.at[j], out_rs.at[p], (dp, p)).wait_recv()
+    gconv_ref[...] = gc_out[...].reshape(64, 1536)
+    for j in range(1, 4):
+        zp = (zpos + j) % 4
+        remote(sm_z.at[zp], sm_z.at[zp], sz_ss.at[j], sz_rs.at[zp], (zp * 2 + ypos, grp)).wait_recv()
+    small_ref[...] = (sm_z[0] + sm_z[1]) + (sm_z[2] + sm_z[3])
+    for c in row_sends + first_sends + conv_sends + forwards + sg + zs + outs + sz:
+        c.wait_send()
+
+
+def local_fused(
+    waveform, lengths, packing, first_weight, norm_gain, norm_bias, conv_weight, grad_features
+):
+    dp = lax.axis_index("dp")
+    masked = jnp.where(jnp.arange(2560)[None, :] < lengths[:, None], waveform, jnp.zeros_like(waveform))
+    blocks = masked.reshape(4, 256, 10).transpose(0, 2, 1)
+    notes = jnp.stack([packing, lengths // 16, lengths % 16], axis=1).astype(BF16)
+    notes = jnp.broadcast_to(notes[:, :, None], (4, 3, 256))
+    wave_rows = jnp.concatenate([blocks, notes, jnp.zeros((4, 3, 256), BF16)], axis=1)
+    turned = first_weight.T
+    gap = lambda rows: jnp.zeros((rows, 64), BF16)
+    stacked = jnp.concatenate(
+        [turned, gap(6), gap(5), turned[0:5], gap(6), turned[5:10], gap(11)], axis=0
+    )
+    odd_half = dp % 2 == 1
+    blank = jnp.zeros_like(stacked)
+    first_rows = jnp.concatenate(
+        [jnp.where(odd_half, blank, stacked), jnp.where(odd_half, stacked, blank)], axis=1
+    )
+    vmem = lambda *shape: pltpu.VMEM(shape, F32)
+    vmem16 = lambda *shape: pltpu.VMEM(shape, BF16)
+    dma = pltpu.SemaphoreType.DMA
+    features, grad_conv, small = pl.pallas_call(
+        fused_kernel,
+        out_shape=(
+            jax.ShapeDtypeStruct((4, 255, 512), BF16),
+            jax.ShapeDtypeStruct((64, 1536), F32),
+            jax.ShapeDtypeStruct((16, 512), F32),
+        ),
+        in_specs=[pl.BlockSpec(memory_space=pltpu.VMEM)] * 6,
+        out_specs=[pl.BlockSpec(memory_space=pltpu.VMEM)] * 3,
+        scratch_shapes=[
+            vmem16(4, 4, 16, 256), vmem16(8, 48, 128), vmem16(32, 1024), vmem16(8, 2, 32, 1536),
+            vmem(4, 256, 1024), vmem(4, 256, 1024), vmem16(1024, 1536), vmem(264, 512),
+            vmem16(1024, 512), vmem(256, 512),
+            vmem16(256, 512), vmem16(256, 512), vmem16(4, 32, 256), vmem(4, 1, 512), vmem(4, 1, 512),
+            vmem(264, 1024), vmem16(256, 1024), vmem(32, 1024), vmem(8, 512),
+            vmem(8, 2, 2, 16, 1536), vmem16(8, 2, 2, 16, 1536), vmem16(8, 2, 16, 1536),
+            vmem(8, 16, 1536), vmem16(8, 16, 1536), vmem16(8, 16, 1536),
+            vmem(4, 16, 1536), vmem16(4, 16, 1536), vmem16(4, 16, 1536),
+            vmem(4, 16, 1536), vmem16(4, 16, 1536), vmem16(4, 16, 1536), vmem(4, 16, 1536),
+            vmem(4, 16, 512), vmem(2, 16, 512), vmem(4, 16, 512),
+            dma((4,)), dma((4,)), dma((8,)), dma((8,)), dma((8,)), dma((8,)), dma((8,)), dma((8,)), dma,
+            dma((3,)), dma((3,)), dma((4,)), dma((4,)), dma((4,)), dma((4,)), dma((4,)), dma((4,)),
+            dma, dma, dma((4,)), dma((4,)),
+        ],
+        compiler_params=pltpu.CompilerParams(
+            collective_id=0, has_side_effects=True, vmem_limit_bytes=60 * 1024 * 1024
+        ),
+    )(wave_rows, first_rows, conv_weight.reshape(2, 32, 1536), norm_gain[None], norm_bias[None], grad_features)
+    grad_first = lax.dynamic_slice_in_dim(small[0:10], dp * 64, 64, 1).T
+    return (features, grad_conv, grad_first, small[10], small[11])
+
+
 def solution(mesh):
+    shape = dict(mesh.shape)
+    fused = shape["dp"] == 8 and shape["group"] == 4
     return jax.shard_map(
-        local,
+        local_fused if fused else local,
         mesh=mesh,
         in_specs=(
             P(("dp", "group"), None),

time: 211 us -> 79.4 us (0.38)
  blocking collectives: 78 us -> 0 us
  Pallas kernels: 0 us -> 65.5 us
  waiting for transfers between devices: 43.6 us -> 0 us
  local copies, waits for them, and re-layouts: 32.4 us -> 11.3 us
  matrix products: 18.5 us -> 0 us
  other arithmetic: 19.6 us -> 1.49 us
  between operations: 14.7 us -> 0.75 us
  starting transfers between devices: 3.57 us -> 0 us
    pallas_call x0 -> x1, Pallas kernels: none -> 65.5 us  [local_fused(): pl.pallas_call(fused_kernel, out_shape=(jax.ShapeDtypeStruct((4, 255, 512...]
    psum x1 -> x0, blocking collectives: 40.1 us -> none  [local(): summed = lax.psum(stacked, ('dp', 'group'))]
    psum x1 -> x0, waiting for transfers between devices: 33.6 us -> none  [local(): grad_conv = lax.psum(share, 'group')]
    all_gather x1 -> x0, blocking collectives: 31.5 us -> none  [local(): first_whole = lax.all_gather(first_weight, 'dp', axis=0, tiled=True)]
    dot_general x9 -> x0, matrix products: 18.5 us -> none  [the longest x1 10.2 us: local(): lax.dot_general(taps_second, conv_whole, (((1,), (1,)), ((), ())), prefer...]
    convert_element_type x4 -> x0, other arithmetic: 10.4 us -> none  [the longest x1 10.2 us: local(): (jax.nn.gelu(shifted, approximate=False) * valid_first).astype(jnp.bfloat16)]
    reduce_scatter x1 -> x0, waiting for transfers between devices: 9.35 us -> none  [local(): lax.psum_scatter(lax.dot_general(delta_flat, taps_second, (((0,), (0,)),...]
    reshape x3 -> x2, local copies, waits for them, and re-layouts: 9.79 us -> 0.68 us  [local_fused(): blocks = masked.reshape(4, 256, 10).transpose(0, 2, 1)]
  transfers between devices with their start and end apart: 4 -> 0, of which waited for: 2 -> 0; matrix products, arithmetic and copies ran while one was open for 26% -> 0% of each run, Pallas kernels for 0% -> 0%
where the time goes in v1:
time: 79.4 us; the launch traced here: 79 us
  Pallas kernels  65.5 us (82%)
  local copies, waits for them, and re-layouts  11.3 us (14%)
  other arithmetic  1.49 us (2%)
    pallas_call x1, Pallas kernels, local_fused(): pl.pallas_call(fused_kernel, out_shape=(jax.ShapeDtypeStruct((4, 255, 512...  65.5 us
    unnamed x13, local copies, waits for them, and re-layouts  7.36 us

profile of v1, /device:TPU:0, one launch (start us, length us, event | category | flops | bytes accessed | tf_op | source)
XLA Modules:
  0.0 79.0 jit_solution(15097855390375832897)
XLA Ops:
  0.7 0.0 copy-start.3
  0.7 0.0 copy-start.4
  0.7 0.1 pad.4.clone
  0.8 0.6 copy-done.3
  1.3 0.0 copy-done.4
  1.3 0.0 copy-start.2
  1.4 0.1 copy.17
  1.5 0.6 copy-done.2
  2.1 0.3 concatenate.15
  2.3 0.1 broadcast_in_dim.30
  2.4 0.0 copy-start.1
  2.4 0.7 pad_maximum_fusion.first_ref
  3.1 0.0 copy-done.1
  3.1 0.1 fusion
  3.2 0.5 reshape.45
  3.8 0.1 copy.16
  3.9 0.7 maximum_maximum_fusion.wave_ref
  4.6 2.4 %copy.18.cot_ref = bf16[4,255,512]{2,1,0:T(8,128)(2,1)} copy(bf16[4,255,512]{2,0,1:T(4,128)(2,1)} %param.15) | data formatting | bytes 2088960 | tf_op args[7]
  7.0 65.5 %shard_map.119 = (bf16[4,255,512]{2,1,0:T(8,128)(2,1)}, f32[64,1536]{1,0:T(8,128)}, f32[16,512]{1,0:T(8,128)}) custom-call(bf16[4,16,256]{2,1,0:T(8,128)(2,1)} %maximum_maximum_fusion.wave_ref, bf16[48,128]{1,0:T(8,128)(2,1)} %pad_maximum_fusion.first_ref, bf16[2,32,1536]{2,1,0:T(8,128)(2,1)} %bitcast.16, f32[1,512]{1,0:T(1,128)} %bitcast.21, ...), custom_call_target="tpu_custom_call" | custom-call | tf_op jit(solution)/shard_map/pallas_call | solution.py:550
  72.5 0.0 copy-start
  72.5 3.0 %copy.19 = bf16[4,255,512]{2,0,1:T(4,128)(2,1)} copy(bf16[4,255,512]{2,1,0:T(8,128)(2,1)} %get-tuple-element.16) | data formatting | bytes 2088960
  75.5 1.4 %fusion.3 = (f32[1,512]{1,0:T(1,128)}, f32[1,512]{1,0:T(1,128)}) fusion(f32[16,512]{1,0:T(8,128)} %get-tuple-element.10), kind=kLoop, calls=%fused_computation.17 | loop fusion | bytes 8192 | tf_op jit(solution)/shard_map/slice | solution.py:579
  76.9 1.4 %dynamic-slice_bitcast_fusion = f32[64,10]{0,1:T(8,128)} fusion(f32[10,512]{1,0:T(8,128)} %bitcast.20, s32[]{:T(128)S(6)} %select_n.44), kind=kLoop, calls=%fused_computation.6 | loop fusion | bytes 5124 | tf_op jit(solution)/shard_map/transpose | solution.py:578
  78.3 0.0 copy-done
  78.3 0.7 copy.21
  (8 shorter events, 0.1 us)
Async XLA Ops:
  0.7 0.7 copy-start.3
  0.7 0.7 copy-start.4
  1.3 0.7 copy-start.2
  2.4 0.7 copy-start.1
  72.5 5.8 %copy-start = (f32[64,1536]{1,0:T(8,128)S(1)}, f32[64,1536]{1,0:T(8,128)}, u32[]{:S(2)}) copy-start(f32[64,1536]{1,0:T(8,128)} %get-tuple-element.36) | copy-start | bytes 1179652

commit v2 on v1

--- a/solution.py
+++ b/solution.py
@@ -178,6 +178,9 @@
     return (features, grad_conv, grad_first, summed[:, 10], summed[:, 11])
 
 
+WIDTH = 384
+
+
 def phi_and_slope(values):
     phi = 0.5 * (1.0 + lax.erf(values * 0.7071067811865476))
     return phi, phi + values * jnp.exp(-0.5 * values * values) * 0.3989422804014327
@@ -226,12 +229,14 @@
         c = remote(first_ref, first_all.at[dp], first_ss.at[j], first_rs.at[dp], ((dp + j) % 8, grp))
         c.start()
         first_sends.append(c)
-    for j in range(1, 8):
-        c = remote(
-            conv_ref.at[core], conv_all.at[dp, core], conv_ss.at[j], conv_rs.at[dp], ((dp + j) % 8, grp)
-        )
+    for j in range(1, 4):
+        peer = (((zpos + j) % 4) * 2 + ypos, grp)
+        c = remote(conv_ref.at[core], conv_all.at[dp, core], conv_ss.at[j], conv_rs.at[dp], peer)
         c.start()
         conv_sends.append(c)
+    c = remote(conv_ref.at[core], conv_all.at[dp, core], conv_ss.at[0], conv_rs.at[dp], ypeer)
+    c.start()
+    conv_sends.append(c)
     own = pltpu.make_async_copy(conv_ref, conv_all.at[dp], own_sem)
     own.start()
     rows_all[grp] = wave_ref[...]
@@ -324,13 +329,27 @@
         taps[all_rows, 1024:1536] = even_rows[1:257].astype(BF16)
         return 0
 
-    lax.fori_loop(0, 4, front, 0)
+    lax.fori_loop(0, 2, front, 0)
 
     forwards = []
-    for j in range(1, 8):
-        p = (dp + j) % 8
-        remote(conv_ref.at[core], conv_all.at[p, core], conv_ss.at[j], conv_rs.at[p], (p, grp)).wait_recv()
-        c = remote(conv_all.at[p, core], conv_all.at[p, core], fwd_ss.at[j], fwd_rs.at[p], partner)
+    for j in range(1, 4):
+        p = ((zpos + j) % 4) * 2 + ypos
+        piece = conv_all.at[p, core]
+        remote(piece, piece, conv_ss.at[j], conv_rs.at[p], (p, grp)).wait_recv()
+        c = remote(piece, piece, conv_ss.at[3 + j], conv_rs.at[p], ypeer)
+        c.start()
+        forwards.append(c)
+        c = remote(piece, piece, fwd_ss.at[j], fwd_rs.at[p], partner)
+        c.start()
+        forwards.append(c)
+
+    lax.fori_loop(2, 4, front, 0)
+
+    for j in range(4):
+        p = ((zpos + j) % 4) * 2 + 1 - ypos
+        piece = conv_all.at[p, core]
+        remote(piece, piece, conv_ss.at[0], conv_rs.at[p], ypeer).wait_recv()
+        c = remote(piece, piece, fwd_ss.at[4 + j], fwd_rs.at[p], partner)
         c.start()
         forwards.append(c)
     own.wait()
@@ -365,18 +384,100 @@
 
     lax.fori_loop(0, 4, middle, 0)
 
-    def weight_grad(m, _):
-        cols = pl.ds(pl.multiple_of(m * 128, 128), 128)
-        part = lax.dot_general(
-            delta[:, cols], taps[...], (((0,), (0,)), ((), ())), preferred_element_type=F32
-        ).reshape(2, 2, 2, 16, 1536)
-        gc_full[pl.ds(m * 2, 2)] = part
-        gc_send[pl.ds(m * 2, 2)] = part.astype(BF16)
-        return 0
-
-    lax.fori_loop(0, 4, weight_grad, 0)
-    stage1 = remote(gc_send.at[:, :, 1 - core], gc_r1, st_ss.at[0], st_rs.at[0], partner)
-    stage1.start()
+    stage = {}
+
+    def weight_grad(b):
+        def rows_of(m, _):
+            cols = pl.ds(pl.multiple_of(m * 128, 128), 128)
+            part = lax.dot_general(
+                delta[:, cols],
+                taps[:, b * WIDTH : (b + 1) * WIDTH],
+                (((0,), (0,)), ((), ())),
+                preferred_element_type=F32,
+            ).reshape(2, 2, 2, 16, WIDTH)
+            gc_full[b, pl.ds(m * 2, 2)] = part
+            gc_send[b, pl.ds(m * 2, 2)] = part.astype(BF16)
+            return 0
+
+        lax.fori_loop(0, 4, rows_of, 0)
+        stage[b, 0] = remote(gc_send.at[b, :, :, 1 - core], gc_r1.at[b], st_ss.at[b, 0], st_rs.at[b, 0], partner)
+        stage[b, 0].start()
+
+    def reduce_first(b):
+        stage[b, 0].wait()
+
+        def one(i, _):
+            if b % 2 == 0:
+                keep, give = (i, xpos), (i, 1 - xpos)
+            else:
+                keep, give = ((i // 2) * 2 + ypos, i % 2), ((i // 2) * 2 + 1 - ypos, i % 2)
+            gc_k2[b, i] = gc_full[b, keep[0], keep[1], core] + gc_r1[b, keep[0], keep[1]].astype(F32)
+            gc_s2[b, i] = (
+                gc_full[b, give[0], give[1], core] + gc_r1[b, give[0], give[1]].astype(F32)
+            ).astype(BF16)
+            return 0
+
+        lax.fori_loop(0, 8, one, 0)
+        peer = xpeer if b % 2 == 0 else ypeer
+        stage[b, 1] = remote(gc_s2.at[b], gc_r2.at[b], st_ss.at[b, 1], st_rs.at[b, 1], peer)
+        stage[b, 1].start()
+
+    def reduce_second(b):
+        stage[b, 1].wait()
+        place = ypos if b % 2 == 0 else xpos
+
+        def one(z, _):
+            keep, give = z * 2 + place, z * 2 + 1 - place
+            gc_k3[b, z] = gc_k2[b, keep] + gc_r2[b, keep].astype(F32)
+            gc_s3[b, z] = (gc_k2[b, give] + gc_r2[b, give].astype(F32)).astype(BF16)
+            return 0
+
+        lax.fori_loop(0, 4, one, 0)
+        peer = ypeer if b % 2 == 0 else xpeer
+        stage[b, 2] = remote(gc_s3.at[b], gc_r3.at[b], st_ss.at[b, 2], st_rs.at[b, 2], peer)
+        stage[b, 2].start()
+
+    late_sends = []
+
+    def reduce_third(b):
+        stage[b, 2].wait()
+
+        def one(z, _):
+            total = gc_k3[b, z] + gc_r3[b, z].astype(F32)
+            gc_k4[b, z] = total
+            gc_s4[b, z] = total.astype(BF16)
+            return 0
+
+        lax.fori_loop(0, 4, one, 0)
+        for j in range(1, 4):
+            zp = (zpos + j) % 4
+            c = remote(
+                gc_s4.at[b, zp], gc_r4.at[b, zpos], z_ss.at[b, j], z_rs.at[b, zpos], (zp * 2 + ypos, grp)
+            )
+            c.start()
+            late_sends.append(c)
+
+    def reduce_last(b):
+        total = gc_k4[b, zpos]
+        for j in range(1, 4):
+            zp = (zpos + j) % 4
+            piece = gc_r4.at[b, zp]
+            remote(piece, piece, z_ss.at[b, j], z_rs.at[b, zp], (zp * 2 + ypos, grp)).wait_recv()
+            total = total + gc_r4[b, zp].astype(F32)
+        gc_out[b, grp] = total.astype(BF16)
+        for j in range(1, 4):
+            c = remote(
+                gc_out.at[b, grp], gc_out.at[b, grp], out_ss.at[b, j], out_rs.at[b, grp], (dp, (grp + j) % 4)
+            )
+            c.start()
+            late_sends.append(c)
+
+    def gathered(b):
+        for j in range(1, 4):
+            p = (grp + j) % 4
+            piece = gc_out.at[b, p]
+            remote(piece, piece, out_ss.at[b, j], out_rs.at[b, p], (dp, p)).wait_recv()
+        gconv_ref[:, b * WIDTH : (b + 1) * WIDTH] = gc_out[b].astype(F32).reshape(64, WIDTH)
 
     def backward(r):
         rows = slice(r * 256, r * 256 + 256)
@@ -428,33 +529,19 @@
             lhs_all[r], dfirst[...], (((1,), (0,)), ((), ())), preferred_element_type=F32
         )
 
+    weight_grad(0)
+    weight_grad(1)
+    weight_grad(2)
+    weight_grad(3)
+    reduce_first(0)
+    reduce_first(1)
     backward(0)
-
-    stage1.wait()
-
-    def reduce_core(d, _):
-        gc_k2[d] = gc_full[d, xpos, core] + gc_r1[d, xpos].astype(F32)
-        gc_s2[d] = (gc_full[d, 1 - xpos, core] + gc_r1[d, 1 - xpos].astype(F32)).astype(BF16)
-        return 0
-
-    lax.fori_loop(0, 8, reduce_core, 0)
-    stage2 = remote(gc_s2, gc_r2, st_ss.at[1], st_rs.at[1], xpeer)
-    stage2.start()
-
+    reduce_first(2)
+    reduce_first(3)
     backward(1)
     backward(2)
-    stage2.wait()
-
-    def reduce_x(z, _):
-        keep, give = z * 2 + ypos, z * 2 + 1 - ypos
-        gc_k3[z] = gc_k2[keep] + gc_r2[keep].astype(F32)
-        gc_s3[z] = (gc_k2[give] + gc_r2[give].astype(F32)).astype(BF16)
-        return 0
-
-    lax.fori_loop(0, 4, reduce_x, 0)
-    stage3 = remote(gc_s3, gc_r3, st_ss.at[2], st_rs.at[2], ypeer)
-    stage3.start()
-
+    reduce_second(0)
+    reduce_second(1)
     backward(3)
 
     small = sm_grp.at[grp]
@@ -463,27 +550,13 @@
     small[5:10] = small[5:10] + first_acc[16:21, 512:1024]
     small[10:12] = sums[0:2]
     small[12:16] = jnp.zeros((4, 512), F32)
-    sg = []
     for j in range(1, 4):
         c = remote(sm_grp.at[grp], sm_grp.at[grp], sg_ss.at[j], sg_rs.at[grp], (dp, (grp + j) % 4))
         c.start()
-        sg.append(c)
-
-    stage3.wait()
-
-    def reduce_y(z, _):
-        total = gc_k3[z] + gc_r3[z].astype(F32)
-        gc_k4[z] = total
-        gc_s4[z] = total.astype(BF16)
-        return 0
-
-    lax.fori_loop(0, 4, reduce_y, 0)
-    zs = []
-    for j in range(1, 4):
-        zp = (zpos + j) % 4
-        c = remote(gc_s4.at[zp], gc_r4.at[zpos], z_ss.at[j], z_rs.at[zpos], (zp * 2 + ypos, grp))
-        c.start()
-        zs.append(c)
+        late_sends.append(c)
+
+    reduce_third(0)
+    reduce_third(1)
 
     for j in range(1, 4):
         p = (grp + j) % 4
@@ -492,36 +565,26 @@
     sy = remote(sm_y.at[0], sm_y.at[1], sy_ss, sy_rs, ypeer)
     sy.start()
 
-    total = gc_k4[zpos]
-    for j in range(1, 4):
-        zp = (zpos + j) % 4
-        remote(gc_s4.at[zp], gc_r4.at[zp], z_ss.at[j], z_rs.at[zp], (zp * 2 + ypos, grp)).wait_recv()
-    for j in range(1, 4):
-        total = total + gc_r4[(zpos + j) % 4].astype(F32)
-    gc_out[grp] = total
-    outs = []
-    for j in range(1, 4):
-        c = remote(gc_out.at[grp], gc_out.at[grp], out_ss.at[j], out_rs.at[grp], (dp, (grp + j) % 4))
-        c.start()
-        outs.append(c)
-
+    reduce_second(2)
+    reduce_second(3)
     sy.wait()
     sm_z[zpos] = sm_y[0] + sm_y[1]
-    sz = []
     for j in range(1, 4):
         zp = (zpos + j) % 4
         c = remote(sm_z.at[zpos], sm_z.at[zpos], sz_ss.at[j], sz_rs.at[zpos], (zp * 2 + ypos, grp))
         c.start()
-        sz.append(c)
-    for j in range(1, 4):
-        p = (grp + j) % 4
-        remote(gc_out.at[p], gc_out.at[p], out_ss.at[j], out_rs.at[p], (dp, p)).wait_recv()
-    gconv_ref[...] = gc_out[...].reshape(64, 1536)
+        late_sends.append(c)
+    reduce_third(2)
+    reduce_third(3)
+    for b in range(4):
+        reduce_last(b)
     for j in range(1, 4):
         zp = (zpos + j) % 4
         remote(sm_z.at[zp], sm_z.at[zp], sz_ss.at[j], sz_rs.at[zp], (zp * 2 + ypos, grp)).wait_recv()
     small_ref[...] = (sm_z[0] + sm_z[1]) + (sm_z[2] + sm_z[3])
-    for c in row_sends + first_sends + conv_sends + forwards + sg + zs + outs + sz:
+    for b in range(4):
+        gathered(b)
+    for c in row_sends + first_sends + conv_sends + forwards + late_sends:
         c.wait_send()
 
 
@@ -562,13 +625,14 @@
             vmem16(1024, 512), vmem(256, 512),
             vmem16(256, 512), vmem16(256, 512), vmem16(4, 32, 256), vmem(4, 1, 512), vmem(4, 1, 512),
             vmem(264, 1024), vmem16(256, 1024), vmem(32, 1024), vmem(8, 512),
-            vmem(8, 2, 2, 16, 1536), vmem16(8, 2, 2, 16, 1536), vmem16(8, 2, 16, 1536),
-            vmem(8, 16, 1536), vmem16(8, 16, 1536), vmem16(8, 16, 1536),
-            vmem(4, 16, 1536), vmem16(4, 16, 1536), vmem16(4, 16, 1536),
-            vmem(4, 16, 1536), vmem16(4, 16, 1536), vmem16(4, 16, 1536), vmem(4, 16, 1536),
+            vmem(4, 8, 2, 2, 16, WIDTH), vmem16(4, 8, 2, 2, 16, WIDTH), vmem16(4, 8, 2, 16, WIDTH),
+            vmem(4, 8, 16, WIDTH), vmem16(4, 8, 16, WIDTH), vmem16(4, 8, 16, WIDTH),
+            vmem(4, 4, 16, WIDTH), vmem16(4, 4, 16, WIDTH), vmem16(4, 4, 16, WIDTH),
+            vmem(4, 4, 16, WIDTH), vmem16(4, 4, 16, WIDTH), vmem16(4, 4, 16, WIDTH),
+            vmem16(4, 4, 16, WIDTH),
             vmem(4, 16, 512), vmem(2, 16, 512), vmem(4, 16, 512),
             dma((4,)), dma((4,)), dma((8,)), dma((8,)), dma((8,)), dma((8,)), dma((8,)), dma((8,)), dma,
-            dma((3,)), dma((3,)), dma((4,)), dma((4,)), dma((4,)), dma((4,)), dma((4,)), dma((4,)),
+            dma((4, 3)), dma((4, 3)), dma((4, 4)), dma((4, 4)), dma((4, 4)), dma((4, 4)), dma((4,)), dma((4,)),
             dma, dma, dma((4,)), dma((4,)),
         ],
         compiler_params=pltpu.CompilerParams(

time: 79.4 us -> 72.9 us (0.918)
  Pallas kernels: 65.5 us -> 58.9 us
    pallas_call x1, Pallas kernels: 65.5 us -> 58.9 us  [local_fused(): pl.pallas_call(fused_kernel, out_shape=(jax.ShapeDtypeStruct((4, 255, 512...]
where the time goes in v2:
time: 72.9 us; the launch traced here: 72.5 us
  Pallas kernels  58.9 us (81%)
  local copies, waits for them, and re-layouts  11.3 us (16%)
  other arithmetic  1.49 us (2%)
  between operations  0.75 us (1%)
    pallas_call x1, Pallas kernels, local_fused(): pl.pallas_call(fused_kernel, out_shape=(jax.ShapeDtypeStruct((4, 255, 512...  58.9 us
    unnamed x13, local copies, waits for them, and re-layouts  7.36 us

profile of v2, /device:TPU:0, one launch (start us, length us, event | category | flops | bytes accessed | tf_op | source)
XLA Modules:
  0.0 72.5 jit_solution(4051036476423480333)
XLA Ops:
  0.7 0.0 copy-start.3
  0.7 0.0 copy-start.4
  0.7 0.1 pad.4.clone
  0.8 0.6 copy-done.3
  1.3 0.0 copy-done.4
  1.3 0.0 copy-start.2
  1.4 0.1 copy.17
  1.5 0.6 copy-done.2
  2.1 0.3 concatenate.15
  2.3 0.1 broadcast_in_dim.30
  2.4 0.0 copy-start.1
  2.4 0.7 pad_maximum_fusion.first_ref
  3.1 0.0 copy-done.1
  3.1 0.1 fusion
  3.2 0.5 reshape.45
  3.8 0.1 copy.16
  3.9 0.7 maximum_maximum_fusion.wave_ref
  4.6 2.4 %copy.18.cot_ref = bf16[4,255,512]{2,1,0:T(8,128)(2,1)} copy(bf16[4,255,512]{2,0,1:T(4,128)(2,1)} %param.15) | data formatting | bytes 2088960 | tf_op args[7]
  7.0 58.9 %shard_map.119 = (bf16[4,255,512]{2,1,0:T(8,128)(2,1)}, f32[64,1536]{1,0:T(8,128)}, f32[16,512]{1,0:T(8,128)}) custom-call(bf16[4,16,256]{2,1,0:T(8,128)(2,1)} %maximum_maximum_fusion.wave_ref, bf16[48,128]{1,0:T(8,128)(2,1)} %pad_maximum_fusion.first_ref, bf16[2,32,1536]{2,1,0:T(8,128)(2,1)} %bitcast.16, f32[1,512]{1,0:T(1,128)} %bitcast.21, ...), custom_call_target="tpu_custom_call" | custom-call | tf_op jit(solution)/shard_map/pallas_call | solution.py:613
  65.9 0.0 copy-start
  65.9 3.0 %copy.19 = bf16[4,255,512]{2,0,1:T(4,128)(2,1)} copy(bf16[4,255,512]{2,1,0:T(8,128)(2,1)} %get-tuple-element.16) | data formatting | bytes 2088960
  69.0 1.4 %fusion.3 = (f32[1,512]{1,0:T(1,128)}, f32[1,512]{1,0:T(1,128)}) fusion(f32[16,512]{1,0:T(8,128)} %get-tuple-element.10), kind=kLoop, calls=%fused_computation.17 | loop fusion | bytes 8192 | tf_op jit(solution)/shard_map/slice | solution.py:643
  70.4 1.4 %dynamic-slice_bitcast_fusion = f32[64,10]{0,1:T(8,128)} fusion(f32[10,512]{1,0:T(8,128)} %bitcast.20, s32[]{:T(128)S(6)} %select_n.44), kind=kLoop, calls=%fused_computation.6 | loop fusion | bytes 5124 | tf_op jit(solution)/shard_map/transpose | solution.py:642
  71.7 0.0 copy-done
  71.7 0.7 %copy.21 = f32[64,1536]{1,0:T(8,128)} copy(f32[64,1536]{1,0:T(8,128)S(1)} %copy-done) | data formatting | bytes 786432
  (8 shorter events, 0.1 us)
Async XLA Ops:
  0.7 0.7 copy-start.3
  0.7 0.7 copy-start.4
  1.3 0.7 copy-start.2
  2.4 0.7 %copy-start.1 = (bf16[4,2560]{1,0:T(4,128)(2,1)S(1)}, bf16[4,2560]{1,0:T(4,128)(2,1)}, u32[]{:S(2)}) copy-start(bf16[4,2560]{1,0:T(4,128)(2,1)} %param.8) | copy-start | bytes 61444
  65.9 5.8 %copy-start = (f32[64,1536]{1,0:T(8,128)S(1)}, f32[64,1536]{1,0:T(8,128)}, u32[]{:S(2)}) copy-start(f32[64,1536]{1,0:T(8,128)} %get-tuple-element.36) | copy-start | bytes 1179652

commit v3 on v2

--- a/solution.py
+++ b/solution.py
@@ -192,12 +192,12 @@
 
 def fused_kernel(
     wave_ref, first_ref, conv_ref, gain_ref, bias_ref, cot_ref,
-    feat_ref, gconv_ref, small_ref,
+    feat_ref, gconv_ref, gfirst_ref, ggain_ref, gbias_ref,
     rows_all, first_all, first_both, conv_all, normed, slope, taps, even_rows, delta, second,
-    cot_rows, feat_rows, lhs_all, counts, inv_all, back, dfirst, first_acc, sums,
+    cot_wide, cot_rows, feat_wide, feat_rows, lhs_all, counts, inv_all, back, dfirst, first_acc, sums,
     gc_full, gc_send, gc_r1, gc_k2, gc_s2, gc_r2, gc_k3, gc_s3, gc_r3, gc_k4, gc_s4, gc_r4, gc_out,
     sm_grp, sm_y, sm_z,
-    row_ss, row_rs, first_ss, first_rs, conv_ss, conv_rs, fwd_ss, fwd_rs, own_sem,
+    row_ss, row_rs, first_ss, first_rs, conv_ss, conv_rs, fwd_ss, fwd_rs, own_sem, cot_sem, feat_sem,
     st_ss, st_rs, z_ss, z_rs, out_ss, out_rs, sg_ss, sg_rs, sy_ss, sy_rs, sz_ss, sz_rs,
 ):
     dp, grp = lax.axis_index("dp"), lax.axis_index("group")
@@ -207,16 +207,40 @@
     xpeer = (dp, (1 - xpos) * 2 + core)
     ypeer = (zpos * 2 + (1 - ypos), grp)
 
+    def chunk(i):
+        return pl.ds(pl.multiple_of(i * STEP, STEP), STEP)
+
+    def frame_ids(i):
+        ids = lax.broadcasted_iota(jnp.int32, (STEP, 512), 0) + i * STEP
+        return ids.astype(F32)
+
+    steps = 256 // STEP
+
     def remote(src, dst, ss, rs, dev):
         return pltpu.make_async_remote_copy(
             src_ref=src, dst_ref=dst, send_sem=ss, recv_sem=rs, device_id=dev, device_id_type=MESH
         )
 
+    cot_in = pltpu.make_async_copy(cot_ref, cot_wide.at[0:255], cot_sem)
+    cot_in.start()
     barrier = pltpu.get_barrier_semaphore()
     for j in range(1, 4):
         pl.semaphore_signal(barrier, inc=1, device_id=(dp, (grp + j) % 4), device_id_type=MESH)
     for j in range(1, 8):
         pl.semaphore_signal(barrier, inc=1, device_id=((dp + j) % 8, grp), device_id_type=MESH)
+    cot_wide[255] = jnp.zeros((4, 512), BF16)
+    even_rows[256:264] = jnp.zeros((8, 512), F32)
+    first_acc[...] = jnp.zeros_like(first_acc)
+    sums[...] = jnp.zeros_like(sums)
+    cot_in.wait()
+
+    def split_rows(i, _):
+        block = cot_wide[chunk(i)].astype(F32)
+        for r in range(4):
+            cot_rows[r, chunk(i)] = block[:, r, :].astype(BF16)
+        return 0
+
+    lax.fori_loop(0, steps, split_rows, 0)
     pl.semaphore_wait(barrier, 10)
 
     row_sends = []
@@ -241,10 +265,6 @@
     own.start()
     rows_all[grp] = wave_ref[...]
     first_all[dp] = first_ref[...]
-    cot_rows[240:256] = jnp.zeros((16, 512), BF16)
-    even_rows[256:264] = jnp.zeros((8, 512), F32)
-    first_acc[...] = jnp.zeros_like(first_acc)
-    sums[...] = jnp.zeros_like(sums)
 
     for j in range(1, 4):
         p = (grp + j) % 4
@@ -259,15 +279,6 @@
         first_both[0:16, lanes] = joined[0:16]
         first_both[16:32, lanes] = jnp.zeros((16, 128), BF16)
         first_both[:, 512 + b * 128 : 640 + b * 128] = joined[16:48]
-
-    def chunk(i):
-        return pl.ds(pl.multiple_of(i * STEP, STEP), STEP)
-
-    def frame_ids(i):
-        ids = lax.broadcasted_iota(jnp.int32, (STEP, 512), 0) + i * STEP
-        return ids.astype(F32)
-
-    steps = 256 // STEP
 
     def front(r, _):
         place = (grp * 4 + r).astype(F32)
@@ -366,20 +377,18 @@
             (((1,), (1,)), ((), ())),
             preferred_element_type=F32,
         )
-        cot_rows[0:255] = cot_ref[r]
         count2 = jnp.floor((counts[r] - 2.5) * 0.5) + 1.0
 
         def activate(i, _):
             valid = frame_ids(i) < count2
             value = second[chunk(i)]
             phi, grad = phi_and_slope(value)
-            feat_rows[chunk(i)] = jnp.where(valid, value * phi, 0.0).astype(BF16)
+            feat_rows[r, chunk(i)] = jnp.where(valid, value * phi, 0.0).astype(BF16)
             rows = pl.ds(pl.multiple_of(r * 256 + i * STEP, STEP), STEP)
-            delta[rows, :] = jnp.where(valid, cot_rows[chunk(i)].astype(F32) * grad, 0.0).astype(BF16)
+            delta[rows, :] = jnp.where(valid, cot_rows[r, chunk(i)].astype(F32) * grad, 0.0).astype(BF16)
             return 0
 
         lax.fori_loop(0, steps, activate, 0)
-        feat_ref[r] = feat_rows[0:255]
         return 0
 
     lax.fori_loop(0, 4, middle, 0)
@@ -535,6 +544,15 @@
     weight_grad(3)
     reduce_first(0)
     reduce_first(1)
+
+    def join_rows(i, _):
+        parts = [feat_rows[r, chunk(i)].astype(F32) for r in range(4)]
+        feat_wide[chunk(i)] = jnp.stack(parts, axis=1).astype(BF16)
+        return 0
+
+    lax.fori_loop(0, steps, join_rows, 0)
+    feat_out = pltpu.make_async_copy(feat_wide.at[0:255], feat_ref, feat_sem)
+    feat_out.start()
     backward(0)
     reduce_first(2)
     reduce_first(3)
@@ -581,9 +599,13 @@
     for j in range(1, 4):
         zp = (zpos + j) % 4
         remote(sm_z.at[zp], sm_z.at[zp], sz_ss.at[j], sz_rs.at[zp], (zp * 2 + ypos, grp)).wait_recv()
-    small_ref[...] = (sm_z[0] + sm_z[1]) + (sm_z[2] + sm_z[3])
+    small_sum = (sm_z[0] + sm_z[1]) + (sm_z[2] + sm_z[3])
+    ggain_ref[...] = small_sum[10:11]
+    gbias_ref[...] = small_sum[11:12]
+    gfirst_ref[...] = pltpu.roll(small_sum, (8 - dp) % 8 * 64, 1)[0:10, 0:64]
     for b in range(4):
         gathered(b)
+    feat_out.wait()
     for c in row_sends + first_sends + conv_sends + forwards + late_sends:
         c.wait_send()
 
@@ -610,20 +632,22 @@
     vmem = lambda *shape: pltpu.VMEM(shape, F32)
     vmem16 = lambda *shape: pltpu.VMEM(shape, BF16)
     dma = pltpu.SemaphoreType.DMA
-    features, grad_conv, small = pl.pallas_call(
+    features, grad_conv, grad_first, grad_gain, grad_bias = pl.pallas_call(
         fused_kernel,
         out_shape=(
-            jax.ShapeDtypeStruct((4, 255, 512), BF16),
+            jax.ShapeDtypeStruct((255, 4, 512), BF16),
             jax.ShapeDtypeStruct((64, 1536), F32),
-            jax.ShapeDtypeStruct((16, 512), F32),
+            jax.ShapeDtypeStruct((10, 64), F32),
+            jax.ShapeDtypeStruct((1, 512), F32),
+            jax.ShapeDtypeStruct((1, 512), F32),
         ),
-        in_specs=[pl.BlockSpec(memory_space=pltpu.VMEM)] * 6,
-        out_specs=[pl.BlockSpec(memory_space=pltpu.VMEM)] * 3,
+        in_specs=[pl.BlockSpec(memory_space=pltpu.VMEM)] * 5 + [pl.BlockSpec(memory_space=pl.ANY)],
+        out_specs=[pl.BlockSpec(memory_space=pl.ANY)] + [pl.BlockSpec(memory_space=pltpu.VMEM)] * 4,
         scratch_shapes=[
             vmem16(4, 4, 16, 256), vmem16(8, 48, 128), vmem16(32, 1024), vmem16(8, 2, 32, 1536),
             vmem(4, 256, 1024), vmem(4, 256, 1024), vmem16(1024, 1536), vmem(264, 512),
             vmem16(1024, 512), vmem(256, 512),
-            vmem16(256, 512), vmem16(256, 512), vmem16(4, 32, 256), vmem(4, 1, 512), vmem(4, 1, 512),
+            vmem16(256, 4, 512), vmem16(4, 256, 512), vmem16(256, 4, 512), vmem16(4, 256, 512), vmem16(4, 32, 256), vmem(4, 1, 512), vmem(4, 1, 512),
             vmem(264, 1024), vmem16(256, 1024), vmem(32, 1024), vmem(8, 512),
             vmem(4, 8, 2, 2, 16, WIDTH), vmem16(4, 8, 2, 2, 16, WIDTH), vmem16(4, 8, 2, 16, WIDTH),
             vmem(4, 8, 16, WIDTH), vmem16(4, 8, 16, WIDTH), vmem16(4, 8, 16, WIDTH),
@@ -631,16 +655,15 @@
             vmem(4, 4, 16, WIDTH), vmem16(4, 4, 16, WIDTH), vmem16(4, 4, 16, WIDTH),
             vmem16(4, 4, 16, WIDTH),
             vmem(4, 16, 512), vmem(2, 16, 512), vmem(4, 16, 512),
-            dma((4,)), dma((4,)), dma((8,)), dma((8,)), dma((8,)), dma((8,)), dma((8,)), dma((8,)), dma,
+            dma((4,)), dma((4,)), dma((8,)), dma((8,)), dma((8,)), dma((8,)), dma((8,)), dma((8,)), dma, dma, dma,
             dma((4, 3)), dma((4, 3)), dma((4, 4)), dma((4, 4)), dma((4, 4)), dma((4, 4)), dma((4,)), dma((4,)),
             dma, dma, dma((4,)), dma((4,)),
         ],
         compiler_params=pltpu.CompilerParams(
             collective_id=0, has_side_effects=True, vmem_limit_bytes=60 * 1024 * 1024
         ),
-    )(wave_rows, first_rows, conv_weight.reshape(2, 32, 1536), norm_gain[None], norm_bias[None], grad_features)
-    grad_first = lax.dynamic_slice_in_dim(small[0:10], dp * 64, 64, 1).T
-    return (features, grad_conv, grad_first, small[10], small[11])
+    )(wave_rows, first_rows, conv_weight.reshape(2, 32, 1536), norm_gain[None], norm_bias[None], grad_features.transpose(1, 0, 2))
+    return (features.transpose(1, 0, 2), grad_conv, grad_first.T, grad_gain[0], grad_bias[0])
 
 
 def solution(mesh):

time: 72.9 us -> 70 us (0.960)
  local copies, waits for them, and re-layouts: 11.3 us -> 7.69 us
  Pallas kernels: 58.9 us -> 59.7 us
    slice x1 -> x0, local copies, waits for them, and re-layouts: 1.38 us -> none  [local_fused(): return (features, grad_conv, grad_first, small[10], small[11])]
    transpose x1 -> x0, local copies, waits for them, and re-layouts: 1.37 us -> none  [local_fused(): grad_first = lax.dynamic_slice_in_dim(small[0:10], dp * 64, 64, 1).T]
    unnamed x13 -> x21, local copies, waits for them, and re-layouts: 7.36 us -> 6.47 us
    pallas_call x1, Pallas kernels: 58.9 us -> 59.7 us  [local_fused(): pl.pallas_call(fused_kernel, out_shape=(jax.ShapeDtypeStruct((255, 4, 512...]
where the time goes in v3:
time: 70 us; the launch traced here: 69.6 us
  Pallas kernels  59.7 us (85%)
  local copies, waits for them, and re-layouts  7.69 us (11%)
  other arithmetic  1.49 us (2%)
  between operations  0.75 us (1%)
    pallas_call x1, Pallas kernels, local_fused(): pl.pallas_call(fused_kernel, out_shape=(jax.ShapeDtypeStruct((255, 4, 512...  59.7 us
    unnamed x21, local copies, waits for them, and re-layouts  6.47 us

profile of v3, /device:TPU:0, one launch (start us, length us, event | category | flops | bytes accessed | tf_op | source)
XLA Modules:
  0.0 69.6 jit_solution(4192565678984758217)
XLA Ops:
  0.7 0.0 copy-start.6
  0.7 0.0 copy-start.7
  0.7 0.1 pad.4.clone
  0.8 0.6 copy-done.6
  1.3 0.0 copy-done.7
  1.3 0.0 copy-start.2
  1.4 0.1 copy.15
  1.5 0.6 copy-done.2
  2.1 0.3 concatenate.15
  2.3 0.1 broadcast_in_dim.30
  2.4 0.0 copy-start.1
  2.4 0.7 pad_maximum_fusion.first_ref
  3.1 0.0 copy-done.1
  3.1 0.1 fusion
  3.2 0.5 reshape.45
  3.8 0.1 copy.14
  3.9 0.7 %maximum_maximum_fusion.wave_ref = bf16[4,16,256]{2,1,0:T(8,128)(2,1)} fusion(bf16[4,3,256]{2,1,0:T(4,128)(2,1)S(1)} %broadcast_in_dim.30, bf16[4,10,256]{2,1,0:T(8,128)(2,1)S(1)} %bitcast.19, bf16[16]{0:T(256)(128)(2,1)S(1)} %pad.4.clone), kind=kLoop, calls=%fused_computation.2 | loop fusion | flops 98304 | bytes 59424 | tf_op jit(solution)/shard_map/concatenate | solution.py:621
  4.6 59.7 %shard_map.119 = (bf16[255,4,512]{2,1,0:T(4,128)(2,1)}, f32[64,1536]{1,0:T(8,128)}, f32[10,64]{1,0:T(8,128)}, f32[1,512]{1,0:T(1,128)}, f32[1,512]{1,0:T(1,128)}) custom-call(bf16[4,16,256]{2,1,0:T(8,128)(2,1)} %maximum_maximum_fusion.wave_ref, bf16[48,128]{1,0:T(8,128)(2,1)} %pad_maximum_fusion.first_ref, bf16[2,32,1536]{2,1,0:T(8,128)(2,1)} %bitcast.18, ...), custom_call_target="tpu_custom_call" | custom-call | tf_op jit(solution)/shard_map/pallas_call | solution.py:635
  64.3 0.0 copy-start
  64.3 2.6 %copy.21 = bf16[4,255,512]{2,0,1:T(4,128)(2,1)} copy(bf16[4,255,512]{2,0,1:T(4,128)(2,1)} %bitcast.17) | data formatting | bytes 2088960
  66.9 0.0 copy-done
  66.9 0.0 copy-start.3
  66.9 0.7 %copy.22 = f32[64,1536]{1,0:T(8,128)} copy(f32[64,1536]{1,0:T(8,128)S(1)} %copy-done) | data formatting | bytes 786432
  67.7 0.0 copy-done.3
  67.7 0.0 copy-start.5
  67.7 0.6 copy.23
  68.3 0.1 copy-done.5
  68.4 0.0 copy-start.4
  68.4 0.6 copy.24
  68.9 0.1 copy-done.4
  69.0 0.6 copy.25
  (8 shorter events, 0.1 us)
Async XLA Ops:
  0.7 0.7 copy-start.6
  0.7 0.7 copy-start.7
  1.3 0.7 copy-start.2
  2.4 0.7 %copy-start.1 = (bf16[4,2560]{1,0:T(4,128)(2,1)S(1)}, bf16[4,2560]{1,0:T(4,128)(2,1)}, u32[]{:S(2)}) copy-start(bf16[4,2560]{1,0:T(4,128)(2,1)} %param.8) | copy-start | bytes 61444
  64.3 2.6 %copy-start = (f32[64,1536]{1,0:T(8,128)S(1)}, f32[64,1536]{1,0:T(8,128)}, u32[]{:S(2)}) copy-start(f32[64,1536]{1,0:T(8,128)} %get-tuple-element.28) | copy-start | bytes 1179652
  66.9 0.8 %copy-start.3 = (f32[10,64]{1,0:T(8,128)S(1)}, f32[10,64]{1,0:T(8,128)}, u32[]{:S(2)}) copy-start(f32[10,64]{1,0:T(8,128)} %get-tuple-element.12) | copy-start | bytes 7684
  67.7 0.7 copy-start.5
  68.4 0.7 copy-start.4

commit v4 on v3

--- a/solution.py
+++ b/solution.py
@@ -540,10 +540,11 @@
 
     weight_grad(0)
     weight_grad(1)
+    reduce_first(0)
     weight_grad(2)
+    reduce_first(1)
     weight_grad(3)
-    reduce_first(0)
-    reduce_first(1)
+    reduce_first(2)
 
     def join_rows(i, _):
         parts = [feat_rows[r, chunk(i)].astype(F32) for r in range(4)]
@@ -554,12 +555,11 @@
     feat_out = pltpu.make_async_copy(feat_wide.at[0:255], feat_ref, feat_sem)
     feat_out.start()
     backward(0)
-    reduce_first(2)
     reduce_first(3)
     backward(1)
-    backward(2)
     reduce_second(0)
     reduce_second(1)
+    backward(2)
     backward(3)
 
     small = sm_grp.at[grp]
@@ -608,6 +608,25 @@
     feat_out.wait()
     for c in row_sends + first_sends + conv_sends + forwards + late_sends:
         c.wait_send()
+
+
+def pass_on(*refs):
+    sources, targets, buffers, (in_sem, out_sem) = refs[0:5], refs[5:10], refs[10:15], refs[15:17]
+    spans = [(0, pl.ds(0, 64)), (0, pl.ds(64, 64)), (0, pl.ds(128, 64)), (0, pl.ds(192, 63))]
+    views = [tuple(group[k].at[span] for group in (sources, buffers, targets)) for k, span in spans]
+    views += [(sources[k], buffers[k], targets[k]) for k in range(1, 5)]
+    reads, writes = [], []
+    for k, (source, buffer, target) in enumerate(views):
+        c = pltpu.make_async_copy(source, buffer, in_sem.at[k])
+        c.start()
+        reads.append(c)
+    for k, (source, buffer, target) in enumerate(views):
+        reads[k].wait()
+        c = pltpu.make_async_copy(buffer, target, out_sem.at[k])
+        c.start()
+        writes.append(c)
+    for c in writes:
+        c.wait()
 
 
 def local_fused(
@@ -663,6 +682,14 @@
             collective_id=0, has_side_effects=True, vmem_limit_bytes=60 * 1024 * 1024
         ),
     )(wave_rows, first_rows, conv_weight.reshape(2, 32, 1536), norm_gain[None], norm_bias[None], grad_features.transpose(1, 0, 2))
+    results = (features, grad_conv, grad_first, grad_gain, grad_bias)
+    features, grad_conv, grad_first, grad_gain, grad_bias = pl.pallas_call(
+        pass_on,
+        out_shape=tuple(jax.ShapeDtypeStruct(each.shape, each.dtype) for each in results),
+        in_specs=[pl.BlockSpec(memory_space=pl.ANY)] * 5,
+        out_specs=[pl.BlockSpec(memory_space=pl.ANY)] * 5,
+        scratch_shapes=[pltpu.VMEM(each.shape, each.dtype) for each in results] + [dma((8,)), dma((8,))],
+    )(*results)
     return (features.transpose(1, 0, 2), grad_conv, grad_first.T, grad_gain[0], grad_bias[0])
 
 

time: 70 us -> 67.4 us (0.963)
  local copies, waits for them, and re-layouts: 7.69 us -> 2.4 us
  Pallas kernels: 59.7 us -> 62.4 us
    unnamed x21 -> x8, local copies, waits for them, and re-layouts: 6.47 us -> 1.18 us
    pallas_call x0 -> x1, Pallas kernels: none -> 2.21 us  [local_fused(): pl.pallas_call(pass_on, out_shape=tuple((jax.ShapeDtypeStruct(each.shape,...]
where the time goes in v4:
time: 67.4 us; the launch traced here: 67.1 us
  Pallas kernels  62.4 us (93%)
  local copies, waits for them, and re-layouts  2.4 us (4%)
  other arithmetic  1.49 us (2%)
  between operations  0.74 us (1%)
    pallas_call x1, Pallas kernels, local_fused(): pl.pallas_call(fused_kernel, out_shape=(jax.ShapeDtypeStruct((255, 4, 512...  60.2 us
    pallas_call x1, Pallas kernels, local_fused(): pl.pallas_call(pass_on, out_shape=tuple((jax.ShapeDtypeStruct(each.shape,...  2.21 us

profile of v4, /device:TPU:0, one launch (start us, length us, event | category | flops | bytes accessed | tf_op | source)
XLA Modules:
  0.0 67.1 jit_solution(15983401845536101904)
XLA Ops:
  0.7 0.0 copy-start.2
  0.7 0.0 copy-start.3
  0.7 0.1 pad.4.clone
  0.8 0.6 copy-done.2
  1.3 0.0 copy-done.3
  1.3 0.0 copy-start.1
  1.4 0.1 copy.15
  1.5 0.6 copy-done.1
  2.1 0.3 concatenate.15
  2.3 0.1 broadcast_in_dim.30
  2.4 0.0 copy-start
  2.4 0.7 %pad_maximum_fusion.first_ref = bf16[48,128]{1,0:T(8,128)(2,1)} fusion(bf16[48,64]{1,0:T(8,128)(2,1)S(1)} %get-tuple-element.26, bf16[48,64]{1,0:T(8,128)(2,1)S(1)} %get-tuple-element.25), kind=kLoop, calls=%fused_computation.3 | loop fusion | flops 24576 | bytes 24576 | tf_op jit(solution)/shard_map/concatenate | solution.py:648
  3.1 0.0 copy-done
  3.1 0.1 fusion
  3.2 0.5 reshape.45
  3.8 0.1 copy.14
  3.9 0.7 %maximum_maximum_fusion.wave_ref = bf16[4,16,256]{2,1,0:T(8,128)(2,1)} fusion(bf16[4,3,256]{2,1,0:T(4,128)(2,1)S(1)} %broadcast_in_dim.30, bf16[4,10,256]{2,1,0:T(8,128)(2,1)S(1)} %bitcast.18, bf16[16]{0:T(256)(128)(2,1)S(1)} %pad.4.clone), kind=kLoop, calls=%fused_computation.2 | loop fusion | flops 98304 | bytes 59424 | tf_op jit(solution)/shard_map/concatenate | solution.py:640
  4.6 60.2 %shard_map.119 = (bf16[255,4,512]{2,1,0:T(4,128)(2,1)}, f32[64,1536]{1,0:T(8,128)}, f32[10,64]{1,0:T(8,128)}, f32[1,512]{1,0:T(1,128)}, f32[1,512]{1,0:T(1,128)}) custom-call(bf16[4,16,256]{2,1,0:T(8,128)(2,1)} %maximum_maximum_fusion.wave_ref, bf16[48,128]{1,0:T(8,128)(2,1)} %pad_maximum_fusion.first_ref, bf16[2,32,1536]{2,1,0:T(8,128)(2,1)} %bitcast.17, ...), custom_call_target="tpu_custom_call" | custom-call | tf_op jit(solution)/shard_map/pallas_call | solution.py:654
  64.8 2.2 %shard_map.120 = (bf16[255,4,512]{2,1,0:T(4,128)(2,1)}, f32[64,1536]{1,0:T(8,128)}, f32[10,64]{1,0:T(8,128)}, f32[1,512]{1,0:T(1,128)}, f32[1,512]{1,0:T(1,128)}) custom-call(bf16[255,4,512]{2,1,0:T(4,128)(2,1)} %get-tuple-element.15.refs_0_, f32[64,1536]{1,0:T(8,128)} %get-tuple-element.16.refs_1_, f32[10,64]{1,0:T(8,128)} %get-tuple-element.17.refs_2_, ...), custom_call_target="tpu_custom_call" | custom-call | tf_op jit(solution)/shard_map/pallas_call | solution.py:686
  (8 shorter events, 0.1 us)
Async XLA Ops:
  0.7 0.7 copy-start.2
  0.7 0.7 copy-start.3
  1.3 0.7 %copy-start.1 = (bf16[64,10]{0,1:T(8,128)(2,1)S(1)}, bf16[64,10]{0,1:T(8,128)(2,1)}, u32[]{:S(2)}) copy-start(bf16[64,10]{0,1:T(8,128)(2,1)} %param.11) | copy-start | bytes 3844
  2.4 0.7 %copy-start = (bf16[4,2560]{1,0:T(4,128)(2,1)S(1)}, bf16[4,2560]{1,0:T(4,128)(2,1)}, u32[]{:S(2)}) copy-start(bf16[4,2560]{1,0:T(4,128)(2,1)} %param.8) | copy-start | bytes 61444
